TPU v7x, 128 devices: a whole 4x4x4 slice. The times are simulated.
128 devices in a mesh: section: 4 (over y_hi, core), seq: 32 (over y_lo, x, z).
Axes of the slice: x: 4, y: 4 (y_hi: 2, y_lo: 2; y = y_hi * 2 + y_lo), z: 4, core: 2. Of those that a mesh axis runs over, the one named last changes fastest.
Arguments:
- activations: bfloat16 [4, 4352, 1024], P('section', 'seq'), may hold values from -60 to 60
- incoming: bfloat16 [4, 4352, 1024], P('section', 'seq'), may hold values from -6 to 6
- w_query: bfloat16 [4, 1024, 512], P('section'), may hold values from -0.1875 to 0.1875
- w_key: bfloat16 [4, 1024, 512], P('section'), may hold values from -0.1875 to 0.1875
- w_value: bfloat16 [4, 1024, 512], P('section'), may hold values from -0.1875 to 0.1875
- w_out: bfloat16 [4, 512, 2048], P('section'), may hold values from -0.25 to 0.25
- block_ids: int32 [4352], replicated, may hold values from 0 to 135, never falling along the last dimension, each value on 1 to 256 neighbouring positions
- flip_order: int32 [4, 136], P('section'), may hold values from 0 to 135, each once within a row
Outputs:
- carry_out: bfloat16 [4, 4352, 1024], P('section', 'seq')
- grad_query: float32 [4, 1024, 512], P('section', 'seq')
- grad_key: float32 [4, 1024, 512], P('section', 'seq')
- grad_value: float32 [4, 1024, 512], P('section', 'seq')
- grad_out: float32 [4, 512, 2048], P('section', 'seq')
Inputs may be any that keep to these rules, and one draw needn't show every extreme that they name: `block_ids`: block ids never fall along the sequence; each block holds 1 to 256 tokens, one exactly 256. `flip_order`: each row is a permutation.
All inputs are finite; a program needn't handle non-finite values.
Results may differ from a plain program's by a relative error of at most 0.03.
Values may be sent and summed in bfloat16 or wider, within the bound.
A program may use at most 128 MiB of HBM per device.

v0:
```python
import jax
import jax.numpy as jnp
from jax import lax
from jax.sharding import PartitionSpec as P

HEADS = 8
HEAD_DIM = 64
EPSILON = 1e-06


def partner(block, axis, stride):
    count = lax.axis_size(axis)
    route = []
    for low in range(count):
        high = low | 1 << stride
        if high != low and high < count:
            route += [(low, high), (high, low)]
    return lax.ppermute(block, axis, route)


def shifted(block, axis, distance):
    devices = range(lax.axis_size(axis))
    route = [(i - distance, i) for i in devices if i - distance in devices]
    return lax.ppermute(block, axis, route)


def split_heads(matrix):
    return matrix.reshape(matrix.shape[0], HEADS, HEAD_DIM)


def head_major(matrix):
    return jnp.transpose(split_heads(matrix), (1, 0, 2))


def unit_heads(projected):
    parts = split_heads(projected)
    factor = lax.rsqrt(jnp.mean(parts * parts, axis=-1, keepdims=True) + EPSILON)
    return (parts * factor, factor)


def unit_back(grad_heads, unit, factor):
    return factor * (grad_heads - unit * jnp.mean(grad_heads * unit, axis=-1, keepdims=True))


def mirror(rows):
    for bit in range(lax.axis_size("seq").bit_length() - 1):
        rows = partner(rows, "seq", bit)
    return rows


def to_previous(rows):
    return shifted(rows, "section", -1)


def shards(activations, incoming, w_query, w_key, w_value, w_out, block_ids, flip_order):
    field = activations[0].astype(jnp.float32)
    upstream = incoming[0].astype(jnp.float32)
    weight_query = w_query[0]
    weight_key = w_key[0]
    weight_value = w_value[0]
    weight_out = w_out[0]
    flip_row = flip_order[0]
    rows = field.shape[0]
    width = field.shape[1]
    inner = weight_query.shape[1]
    scale = HEAD_DIM ** (-0.5)
    first = lax.axis_index("seq") * rows
    my_blocks = lax.dynamic_slice_in_dim(block_ids, first, rows)
    row_scale = lax.rsqrt(jnp.mean(field * field, axis=-1, keepdims=True) + EPSILON)
    unit_rows = field * row_scale
    normed = unit_rows.astype(jnp.bfloat16)
    query_raw = jnp.dot(normed, weight_query, preferred_element_type=jnp.float32)
    key_raw = jnp.dot(normed, weight_key, preferred_element_type=jnp.float32)
    values = jnp.dot(normed, weight_value, preferred_element_type=jnp.float32).astype(jnp.bfloat16)
    query_unit, query_scale = unit_heads(query_raw)
    key_unit, key_scale = unit_heads(key_raw)
    queries = query_unit.astype(jnp.bfloat16).reshape(rows, inner)
    keys = key_unit.astype(jnp.bfloat16).reshape(rows, inner)
    keys_all, values_all = (
        lax.all_gather(keys, "seq", axis=0, tiled=True),
        lax.all_gather(values, "seq", axis=0, tiled=True),
    )
    allowed = block_ids[None, :] <= my_blocks[:, None]
    query_heads = head_major(queries)
    key_heads_all = head_major(keys_all)
    value_heads_all = head_major(values_all)

    def probabilities(query_part, key_part):
        scores = jnp.dot(query_part, key_part.T, preferred_element_type=jnp.float32) * scale
        numerator = jnp.where(allowed, jnp.exp(scores), 0.0)
        denominator = jnp.sum(numerator, axis=-1, keepdims=True)
        return (numerator / denominator, denominator)

    def forward_head(operands):
        query_part, key_part, value_part = operands
        probs, denominator = probabilities(query_part, key_part)
        out_part = jnp.dot(
            probs.astype(jnp.bfloat16), value_part, preferred_element_type=jnp.float32
        ).astype(jnp.bfloat16)
        return (out_part, denominator[:, 0])

    heads_out, denominators = lax.map(forward_head, (query_heads, key_heads_all, value_heads_all))
    attended = jnp.transpose(heads_out, (1, 0, 2)).reshape(rows, inner)
    affine = jnp.dot(attended, weight_out, preferred_element_type=jnp.float32)
    shift_part = affine[:, :width]
    log_scale = affine[:, width:]
    factor = jnp.exp(-log_scale)
    latent = (field - shift_part) * factor
    grad_affine = jnp.concatenate([-upstream * factor, 1.0 - upstream * latent], axis=-1).astype(
        jnp.bfloat16
    )
    out_term = jnp.dot(attended.T, grad_affine, preferred_element_type=jnp.float32)
    grad_attn = jnp.dot(grad_affine, weight_out.T, preferred_element_type=jnp.float32).astype(
        jnp.bfloat16
    )
    correction = jnp.sum(
        split_heads(grad_attn.astype(jnp.float32)) * split_heads(attended.astype(jnp.float32)),
        axis=-1,
    )
    grad_heads = head_major(grad_attn)
    correction_heads = jnp.transpose(correction)[:, :, None]

    def backward_head(operands):
        query_part, key_part, value_part, grad_part, corr_part = operands
        probs, denominator = probabilities(query_part, key_part)
        grad_probs = jnp.dot(grad_part, value_part.T, preferred_element_type=jnp.float32)
        grad_scores = (probs * (grad_probs - corr_part)).astype(jnp.bfloat16)
        grad_qpart = jnp.dot(grad_scores, key_part, preferred_element_type=jnp.float32) * scale
        grad_kpart = jnp.dot(grad_scores.T, query_part, preferred_element_type=jnp.float32) * scale
        grad_vpart = jnp.dot(
            probs.astype(jnp.bfloat16).T, grad_part, preferred_element_type=jnp.float32
        )
        return (grad_qpart, grad_kpart, grad_vpart)

    grad_qheads, grad_kall, grad_vall = lax.map(
        backward_head, (query_heads, key_heads_all, value_heads_all, grad_heads, correction_heads)
    )
    key_terms = jnp.transpose(grad_kall, (1, 0, 2)).reshape(-1, inner)
    value_terms = jnp.transpose(grad_vall, (1, 0, 2)).reshape(-1, inner)
    grad_kunit, grad_vsum = (
        lax.psum_scatter(
            key_terms.astype(jnp.bfloat16), "seq", scatter_dimension=0, tiled=True
        ).astype(jnp.float32),
        lax.psum_scatter(
            value_terms.astype(jnp.bfloat16), "seq", scatter_dimension=0, tiled=True
        ).astype(jnp.float32),
    )
    grad_queries = (
        unit_back(jnp.transpose(grad_qheads, (1, 0, 2)), query_unit, query_scale)
        .reshape(rows, inner)
        .astype(jnp.bfloat16)
    )
    grad_keys = (
        unit_back(split_heads(grad_kunit), key_unit, key_scale)
        .reshape(rows, inner)
        .astype(jnp.bfloat16)
    )
    grad_values = grad_vsum.astype(jnp.bfloat16)
    query_term = jnp.dot(normed.T, grad_queries, preferred_element_type=jnp.float32)
    key_term = jnp.dot(normed.T, grad_keys, preferred_element_type=jnp.float32)
    value_term = jnp.dot(normed.T, grad_values, preferred_element_type=jnp.float32)
    sums = (
        lax.psum_scatter(
            query_term.astype(jnp.bfloat16), "seq", scatter_dimension=0, tiled=True
        ).astype(jnp.float32),
        lax.psum_scatter(
            key_term.astype(jnp.bfloat16), "seq", scatter_dimension=0, tiled=True
        ).astype(jnp.float32),
        lax.psum_scatter(
            value_term.astype(jnp.bfloat16), "seq", scatter_dimension=0, tiled=True
        ).astype(jnp.float32),
        lax.psum_scatter(
            out_term.astype(jnp.bfloat16), "seq", scatter_dimension=0, tiled=True
        ).astype(jnp.float32),
    )
    grad_normed = jnp.dot(grad_queries, weight_query.T, preferred_element_type=jnp.float32)
    grad_normed = grad_normed + jnp.dot(grad_keys, weight_key.T, preferred_element_type=jnp.float32)
    grad_normed = grad_normed + jnp.dot(
        grad_values, weight_value.T, preferred_element_type=jnp.float32
    )
    grad_input = upstream * factor + row_scale * (
        grad_normed - unit_rows * jnp.mean(grad_normed * unit_rows, axis=-1, keepdims=True)
    )
    grad_input = grad_input.astype(jnp.bfloat16)
    moved = mirror(to_previous(grad_input))
    carry = jnp.take(moved, flip_row, axis=0)
    return (carry[None], sums[0][None], sums[1][None], sums[2][None], sums[3][None])


def solution(mesh):
    in_specs = (
        P("section", "seq", None),
        P("section", "seq", None),
        P("section", None, None),
        P("section", None, None),
        P("section", None, None),
        P("section", None, None),
        P(),
        P("section", None),
    )
    out_specs = (
        P("section", "seq", None),
        P("section", "seq", None),
        P("section", "seq", None),
        P("section", "seq", None),
        P("section", "seq", None),
    )
    return jax.shard_map(shards, mesh=mesh, in_specs=in_specs, out_specs=out_specs, check_vma=False)
```

profile of v0, /device:TPU:0, one launch (start us, length us, event | category | flops | bytes accessed | tf_op | source)
XLA Modules:
  0.0 1467.9 jit_solution(6070266999776228398)
XLA Ops:
  8.5 2.3 copy.43
  16.0 2.3 convolution_convert_fusion.4
  22.7 153.8 %all-gather.3.cloned.1.call-done = bf16[4352,512]{1,0:T(8,128)(2,1)} async-done(((bf16[136,512]{1,0:T(8,128)(2,1)}), bf16[4352,512]{1,0:T(8,128)(2,1)}) %all-gather.3.cloned.1.call-update) | async-done | bytes 4456464 | tf_op jit(solution)/shard_map/all_gather | solution.py:80
  176.5 6.5 copy.45
  183.0 9.2 copy.48
  192.2 144.8 %all-gather.5.cloned.1.call-done = bf16[4352,512]{1,0:T(8,128)(2,1)} async-done(((bf16[136,512]{1,0:T(8,128)(2,1)}), bf16[4352,512]{1,0:T(8,128)(2,1)}) %all-gather.5.cloned.1.call-update) | async-done | bytes 4456464 | tf_op jit(solution)/shard_map/all_gather | solution.py:81
  337.1 6.5 copy.46
  343.5 9.2 copy.49
  352.7 31.7 %while.26 = (s32[]{:T(128)}, bf16[8,136,64]{1,2,0:T(8,128)(2,1)S(1)}, bf16[8,136,64]{2,1,0:T(8,128)(2,1)S(1)}, bf16[8,4352,64]{2,1,0:T(8,128)(2,1)}, bf16[8,4352...) while((s32[]{:T(128)}, bf16[8,136,64]{1,2,0:T(8,128)(2,1)S(1)}, ...), condition=%wide.region_5.6_spmd.clone, body=%wide.region_3.5_spmd.clone.sunk | while | flops 155079040 | bytes 7055989 | solution.py:102
  352.7 2.0 fusion.137
  356.7 2.0 fusion.137
  360.7 2.0 fusion.137
  364.6 2.0 fusion.137
  368.6 2.0 fusion.137
  372.5 2.0 fusion.137
  376.5 2.0 fusion.137
  380.5 2.0 fusion.137
  394.2 76.1 %while.27 = (s32[]{:T(128)}, f32[8,136,64]{1,2,0:T(8,128)}, bf16[8,4352,64]{1,2,0:T(8,128)(2,1)}, bf16[8,4352,64]{1,2,0:T(8,128)(2,1)}, bf16[8,136,64]{2,1,0:T(8...) while((s32[]{:T(128)}, f32[8,136,64]{1,2,0:T(8,128)}, ...), condition=%wide.region_9.10_spmd.clone, body=%wide.region_7.9_spmd.clone.sunk | while | flops 385003904 | bytes 16456953 | solution.py:135
  394.2 2.0 fusion.147
  399.3 2.0 fusion.150
  401.3 2.5 fusion.149
  403.8 2.0 fusion.147
  410.8 2.5 fusion.149
  413.2 2.0 fusion.147
  420.2 2.5 fusion.149
  422.7 2.0 fusion.147
  429.7 2.5 fusion.149
  432.2 2.0 fusion.147
  439.3 2.5 fusion.149
  441.8 2.0 fusion.147
  448.8 2.5 fusion.149
  451.3 2.0 fusion.147
  458.3 2.5 fusion.149
  460.8 2.0 fusion.147
  467.8 2.5 fusion.149
  470.3 6.6 copy.56
  476.9 6.5 copy.58
  486.5 2.1 convolution_convert_fusion
  488.8 158.3 %reduce-scatter.19.cloned.1.call-done = bf16[136,512]{1,0:T(8,128)(2,1)} async-done(((bf16[4352,512]{1,0:T(8,128)(2,1)}), bf16[136,512]{1,0:T(8,128)(2,1)}) %reduce-scatter.19.cloned.1.call-update) | async-done | bytes 139280
  653.4 161.8 %reduce-scatter.21.cloned.1.call-done = bf16[136,512]{1,0:T(8,128)(2,1)} async-done(((bf16[4352,512]{1,0:T(8,128)(2,1)}), bf16[136,512]{1,0:T(8,128)(2,1)}) %reduce-scatter.21.cloned.1.call-update) | async-done | bytes 139280
  818.7 2.2 collective-permute-done
  822.5 5.4 collective-permute-done.1
  827.9 8.1 collective-permute-done.2
  836.1 6.9 collective-permute-done.3
  843.0 133.7 %reduce-scatter.11.cloned.1.call-done = bf16[32,512]{1,0:T(8,128)(2,1)} async-done(((bf16[1024,512]{1,0:T(8,128)(2,1)}), bf16[32,512]{1,0:T(8,128)(2,1)}) %reduce-scatter.11.cloned.1.call-update) | async-done | bytes 32784 | tf_op jit(solution)/shard_map/reduce_scatter | solution.py:163
  978.2 161.6 %reduce-scatter.17.cloned.1.call-done = bf16[16,2048]{1,0:T(8,128)(2,1)} async-done(((bf16[512,2048]{1,0:T(8,128)(2,1)}), bf16[16,2048]{1,0:T(8,128)(2,1)}) %reduce-scatter.17.cloned.1.call-update) | async-done | bytes 65552 | tf_op jit(solution)/shard_map/reduce_scatter | solution.py:172
  1143.0 157.0 %reduce-scatter.13.cloned.1.call-done = bf16[32,512]{1,0:T(8,128)(2,1)} async-done(((bf16[1024,512]{1,0:T(8,128)(2,1)}), bf16[32,512]{1,0:T(8,128)(2,1)}) %reduce-scatter.13.cloned.1.call-update) | async-done | bytes 32784 | tf_op jit(solution)/shard_map/reduce_scatter | solution.py:166
  1301.4 158.3 %reduce-scatter.15.cloned.1.call-done = bf16[32,512]{1,0:T(8,128)(2,1)} async-done(((bf16[1024,512]{1,0:T(8,128)(2,1)}), bf16[32,512]{1,0:T(8,128)(2,1)}) %reduce-scatter.15.cloned.1.call-update) | async-done | bytes 32784 | tf_op jit(solution)/shard_map/reduce_scatter | solution.py:169
  (160 shorter events, 95.9 us)
Async XLA Ops:
  7.2 379.8 %copy-start = (bf16[1,512,2048]{2,1,0:T(8,128)(2,1)S(1)}, bf16[1,512,2048]{2,1,0:T(8,128)(2,1)}, u32[]{:S(2)}) copy-start(bf16[1,512,2048]{2,1,0:T(8,128)(2,1)} %param.17) | copy-start | bytes 6291460
  7.2 3.6 copy-start.2
  7.2 169.3 %all-gather.3.cloned.1.call-start = ((), (), s32[]{:S(2)}) async-start(), calls=%async_computation.6 | async-start | bytes 4595712 | tf_op jit(solution)/shard_map/all_gather | solution.py:80
  10.8 7.6 copy-start.7
  12.7 0.8 copy-start.3
  16.0 321.1 %all-gather.5.cloned.1.call-start = ((), (), s32[]{:S(2)}) async-start(), calls=%async_computation.7 | async-start | bytes 4595712 | tf_op jit(solution)/shard_map/all_gather | solution.py:81
  18.3 628.8 %reduce-scatter.19.cloned.1.call-start = ((), (), s32[]{:S(2)}) async-start(), calls=%async_computation.12 | async-start | bytes 4595712
  18.4 4.2 copy-start.23
  21.5 0.8 copy-start.5
  343.5 9.2 copy-start.21
  384.4 0.7 copy-start.19
  385.3 0.7 copy-start.9
  389.5 0.7 copy-start.15
  389.5 0.8 copy-start.17
  476.9 338.3 %reduce-scatter.21.cloned.1.call-start = ((), (), s32[]{:S(2)}) async-start(), calls=%async_computation.13 | async-start | bytes 4595712
  483.4 1.0 copy-start.6
  483.4 1.2 copy-start.12
  483.4 493.3 %reduce-scatter.11.cloned.1.call-start = ((), (), s32[]{:S(2)}) async-start(), calls=%async_computation.8 | async-start | bytes 1081344 | tf_op jit(solution)/shard_map/reduce_scatter | solution.py:163
  484.6 1.8 copy-start.13
  484.6 1.8 copy-start.16
  484.6 1.9 copy-start.18
  486.4 161.8 %copy-start.4 = (f32[136,8,64]{0,2,1:T(8,128)S(1)}, f32[136,8,64]{0,2,1:T(8,128)}, u32[]{:S(2)}) copy-start(f32[136,8,64]{0,2,1:T(8,128)} %copy-done.3) | copy-start | bytes 835588
  486.4 653.4 %reduce-scatter.17.cloned.1.call-start = ((), (), s32[]{:S(2)}) async-start(), calls=%async_computation.11 | async-start | bytes 2162688 | tf_op jit(solution)/shard_map/reduce_scatter | solution.py:172
  488.6 162.2 %copy-start.8 = (bf16[1,1024,512]{2,1,0:T(8,128)(2,1)S(1)}, bf16[1,1024,512]{2,1,0:T(8,128)(2,1)}, u32[]{:S(2)}) copy-start(bf16[1,1024,512]{2,1,0:T(8,128)(2,1)} %param.14) | copy-start | bytes 3145732
  488.6 811.4 %reduce-scatter.13.cloned.1.call-start = ((), (), s32[]{:S(2)}) async-start(), calls=%async_computation.9 | async-start | bytes 1081344 | tf_op jit(solution)/shard_map/reduce_scatter | solution.py:166
  648.4 0.7 copy-start.10
  650.7 0.9 copy-start.11
  650.7 809.0 %reduce-scatter.15.cloned.1.call-start = ((), (), s32[]{:S(2)}) async-start(), calls=%async_computation.10 | async-start | bytes 1081344 | tf_op jit(solution)/shard_map/reduce_scatter | solution.py:169
  651.6 165.5 %copy-start.14 = (bf16[1,136,1024]{2,1,0:T(8,128)(2,1)S(1)}, bf16[1,136,1024]{2,1,0:T(8,128)(2,1)}, u32[]{:S(2)}) copy-start(bf16[1,136,1024]{2,1,0:T(8,128)(2,1)} %param.13) | copy-start | bytes 835588
  815.2 5.7 copy-start.20
  817.1 18.9 %copy-start.22 = (s32[1,136]{1,0:T(1,128)S(1)}, s32[1,136]{1,0:T(1,128)}, u32[]{:S(2)}) copy-start(s32[1,136]{1,0:T(1,128)} %param.19) | copy-start | bytes 1636
  817.4 3.5 collective-permute-start
  820.9 7.0 collective-permute-start.1
  820.9 640.2 %copy-start.1 = (bf16[1,512,2048]{2,1,0:T(8,128)(2,1)S(1)}, bf16[1,512,2048]{2,1,0:T(8,128)(2,1)}, u32[]{:S(2)}) copy-start(bf16[1,512,2048]{2,1,0:T(8,128)(2,1)} %param.17) | copy-start | bytes 6291460
  827.9 8.1 collective-permute-start.2
  836.1 6.9 collective-permute-start.3
  843.0 135.1 %collective-permute-start.4 = (bf16[136,1024]{1,0:T(8,128)(2,1)S(1)}, bf16[136,1024]{1,0:T(8,128)(2,1)S(1)}, u32[]{:S(2)}, u32[]{:S(2)}) collective-permute-start(bf16[136,1024]{1,0:T(8,128)(2,1)S(1)} %collective-permute-done.3), channel_id=1, source_target_pairs={{0,8},{8,0},{1,9},{9,1},{2,10},{10,2},{3,11},{11,3},{4,12},{12,4},... | collective-permute-start | bytes 835592 | tf_op jit(solution)/shard_map/ppermute | solution.py:18
  978.2 163.2 %collective-permute-start.5 = (bf16[136,1024]{1,0:T(8,128)(2,1)S(1)}, bf16[136,1024]{1,0:T(8,128)(2,1)S(1)}, u32[]{:S(2)}, u32[]{:S(2)}) collective-permute-start(bf16[136,1024]{1,0:T(8,128)(2,1)S(1)} %collective-permute-done.4), channel_id=1, source_target_pairs={{0,16},{16,0},{1,17},{17,1},{2,18},{18,2},{3,19},{19,3},{4,20},{20... | collective-permute-start | bytes 835592 | tf_op jit(solution)/shard_map/ppermute | solution.py:18
Sparse Core Ops, SparseCore 0:
  16.1 160.3 all-gather.2
  178.2 158.8 all-gather.4
  477.0 170.0 reduce-scatter.18
  649.5 165.6 reduce-scatter.20
  817.4 159.3 reduce-scatter.10
  979.1 160.6 reduce-scatter.16
  1142.2 157.7 reduce-scatter.12
  1302.4 157.1 reduce-scatter.14
where the time goes:
time: 1470 us
  waiting for transfers between devices  1250 us (85%)
  matrix products  127 us (9%)
  local copies, waits for them, and re-layouts  60.4 us (4%)
    unnamed x10, waiting for transfers between devices  320 us
    reduce_scatter x1, waiting for transfers between devices, shards(): lax.psum_scatter(out_term.astype(jnp.bfloat16), 'seq', scatter_dimension=...  162 us
    reduce_scatter x1, waiting for transfers between devices, shards(): lax.psum_scatter(value_term.astype(jnp.bfloat16), 'seq', scatter_dimensio...  158 us
    reduce_scatter x1, waiting for transfers between devices, shards(): lax.psum_scatter(key_term.astype(jnp.bfloat16), 'seq', scatter_dimension=...  157 us
    all_gather x1, waiting for transfers between devices, shards(): lax.all_gather(keys, 'seq', axis=0, tiled=True)  154 us
    all_gather x1, waiting for transfers between devices, shards(): lax.all_gather(values, 'seq', axis=0, tiled=True)  145 us
    reduce_scatter x1, waiting for transfers between devices, shards(): lax.psum_scatter(query_term.astype(jnp.bfloat16), 'seq', scatter_dimensio...  134 us
    unnamed x58, local copies, waits for them, and re-layouts  42.5 us
  transfers between devices with their start and end apart: 14, of which 12 were waited for; matrix products, arithmetic and copies ran while one was open for 3% of the time, Pallas kernels for 0%

commit v1 on v0

--- a/solution.py
+++ b/solution.py
@@ -78,7 +78,9 @@
     keys = key_unit.astype(jnp.bfloat16).reshape(rows, inner)
     keys_all, values_all = (
         lax.all_gather(keys, "seq", axis=0, tiled=True),
-        lax.all_gather(values, "seq", axis=0, tiled=True),
+        jnp.concatenate(
+            lax.all_to_all(jnp.stack([values] * lax.axis_size("seq")), "seq", 0, 0), axis=0
+        ),
     )
     allowed = block_ids[None, :] <= my_blocks[:, None]
     query_heads = head_major(queries)

time: 1470 us -> 1360 us (0.925)
  waiting for transfers between devices: 1250 us -> 1120 us
    all_gather x1 -> x0, waiting for transfers between devices: 145 us -> none  [shards(): lax.all_gather(values, 'seq', axis=0, tiled=True)]
    all_to_all x0 -> x1, waiting for transfers between devices: none -> 61.4 us  [shards(): lax.all_to_all(jnp.stack([values] * lax.axis_size('seq')), 'seq', 0, 0)]
    all_gather x1, waiting for transfers between devices: 154 us -> 110 us  [shards(): lax.all_gather(keys, 'seq', axis=0, tiled=True)]
    unnamed x58 -> x60, local copies, waits for them, and re-layouts: 42.5 us -> 41.4 us
    unnamed x10 -> x9, waiting for transfers between devices: 320 us -> 320 us
  transfers between devices with their start and end apart: 14 -> 14, of which waited for: 12 -> 12; matrix products, arithmetic and copies ran while one was open for 3% -> 4% of each run, Pallas kernels for 0% -> 0%
where the time goes in v1:
time: 1360 us; the launch traced here: 1350 us
  waiting for transfers between devices  1120 us (82%)
  matrix products  125 us (9%)
  local copies, waits for them, and re-layouts  67.1 us (5%)
  between operations  14.5 us (1%)
    unnamed x9, waiting for transfers between devices  320 us
    reduce_scatter x1, waiting for transfers between devices, shards(): lax.psum_scatter(out_term.astype(jnp.bfloat16), 'seq', scatter_dimension=...  161 us
    reduce_scatter x1, waiting for transfers between devices, shards(): lax.psum_scatter(value_term.astype(jnp.bfloat16), 'seq', scatter_dimensio...  159 us
    reduce_scatter x1, waiting for transfers between devices, shards(): lax.psum_scatter(key_term.astype(jnp.bfloat16), 'seq', scatter_dimension=...  156 us
    reduce_scatter x1, waiting for transfers between devices, shards(): lax.psum_scatter(query_term.astype(jnp.bfloat16), 'seq', scatter_dimensio...  134 us
    all_gather x1, waiting for transfers between devices, shards(): lax.all_gather(keys, 'seq', axis=0, tiled=True)  110 us
    all_to_all x1, waiting for transfers between devices, shards(): lax.all_to_all(jnp.stack([values] * lax.axis_size('seq')), 'seq', 0, 0)  61.4 us
    unnamed x60, local copies, waits for them, and re-layouts  41.4 us
  transfers between devices with their start and end apart: 14, of which 12 were waited for; matrix products, arithmetic and copies ran while one was open for 4% of the time, Pallas kernels for 0%

profile of v1, /device:TPU:0, one launch (start us, length us, event | category | flops | bytes accessed | tf_op | source)
XLA Modules:
  0.0 1353.5 jit_solution(13304122024185574035)
XLA Ops:
  8.5 2.4 copy.42
  16.4 2.3 stack.2
  18.7 9.5 all-to-all-start
  32.6 61.4 %all-to-all-done = bf16[32,136,512]{2,1,0:T(8,128)(2,1)} async-done(((bf16[32,136,512]{2,1,0:T(8,128)(2,1)}), bf16[32,136,512]{2,1,0:T(8,128)(2,1)}, u32[]{:S(2)}, u32[]{:S(2)}) %all-to-all-start) | async-done | bytes 4456480 | tf_op jit(solution)/shard_map/all_to_all | solution.py:82
  94.1 12.1 reshape.215
  106.1 8.1 copy.48
  114.3 109.7 %all-gather.2.cloned.1.call-done = bf16[4352,512]{1,0:T(8,128)(2,1)} async-done(((bf16[136,512]{1,0:T(8,128)(2,1)}), bf16[4352,512]{1,0:T(8,128)(2,1)}) %all-gather.2.cloned.1.call-update) | async-done | bytes 4456464 | tf_op jit(solution)/shard_map/all_gather | solution.py:80
  224.0 6.5 copy.44
  230.4 9.2 copy.47
  239.6 31.7 %while.26 = (s32[]{:T(128)}, bf16[8,136,64]{1,2,0:T(8,128)(2,1)S(1)}, bf16[8,136,64]{2,1,0:T(8,128)(2,1)S(1)}, bf16[8,4352,64]{2,1,0:T(8,128)(2,1)}, bf16[8,4352...) while((s32[]{:T(128)}, bf16[8,136,64]{1,2,0:T(8,128)(2,1)S(1)}, ...), condition=%wide.region_5.6_spmd.clone, body=%wide.region_3.5_spmd.clone.sunk | while | flops 155079040 | bytes 7055989 | solution.py:104
  239.6 2.0 fusion.137
  243.6 2.0 fusion.137
  247.5 2.0 fusion.137
  251.5 2.0 fusion.137
  255.5 2.0 fusion.137
  259.4 2.0 fusion.137
  263.4 2.0 fusion.137
  267.3 2.0 fusion.137
  281.1 76.1 %while.27 = (s32[]{:T(128)}, f32[8,136,64]{1,2,0:T(8,128)}, bf16[8,4352,64]{1,2,0:T(8,128)(2,1)}, bf16[8,4352,64]{1,2,0:T(8,128)(2,1)}, bf16[8,136,64]{2,1,0:T(8...) while((s32[]{:T(128)}, f32[8,136,64]{1,2,0:T(8,128)}, ...), condition=%wide.region_9.10_spmd.clone, body=%wide.region_7.9_spmd.clone.sunk | while | flops 385003904 | bytes 16456953 | solution.py:137
  281.1 2.0 fusion.147
  288.2 2.5 fusion.149
  290.7 2.0 fusion.147
  297.7 2.5 fusion.149
  300.2 2.0 fusion.147
  307.2 2.5 fusion.149
  309.7 2.0 fusion.147
  316.7 2.5 fusion.149
  319.1 2.0 fusion.147
  326.2 2.5 fusion.149
  328.7 2.0 fusion.147
  335.7 2.5 fusion.149
  338.2 2.0 fusion.147
  345.2 2.5 fusion.149
  347.7 2.0 fusion.147
  354.7 2.5 fusion.149
  357.2 6.6 copy.58
  363.8 6.5 copy.60
  373.4 2.1 convolution_convert_fusion
  375.6 157.8 %reduce-scatter.19.cloned.1.call-done = bf16[136,512]{1,0:T(8,128)(2,1)} async-done(((bf16[4352,512]{1,0:T(8,128)(2,1)}), bf16[136,512]{1,0:T(8,128)(2,1)}) %reduce-scatter.19.cloned.1.call-update) | async-done | bytes 139280
  539.6 162.5 %reduce-scatter.21.cloned.1.call-done = bf16[136,512]{1,0:T(8,128)(2,1)} async-done(((bf16[4352,512]{1,0:T(8,128)(2,1)}), bf16[136,512]{1,0:T(8,128)(2,1)}) %reduce-scatter.21.cloned.1.call-update) | async-done | bytes 139280
  705.6 2.2 collective-permute-done
  709.4 5.1 collective-permute-done.1
  714.5 8.1 collective-permute-done.2
  722.7 7.0 collective-permute-done.3
  729.7 134.2 %reduce-scatter.11.cloned.1.call-done = bf16[32,512]{1,0:T(8,128)(2,1)} async-done(((bf16[1024,512]{1,0:T(8,128)(2,1)}), bf16[32,512]{1,0:T(8,128)(2,1)}) %reduce-scatter.11.cloned.1.call-update) | async-done | bytes 32784 | tf_op jit(solution)/shard_map/reduce_scatter | solution.py:165
  865.3 160.6 %reduce-scatter.17.cloned.1.call-done = bf16[16,2048]{1,0:T(8,128)(2,1)} async-done(((bf16[512,2048]{1,0:T(8,128)(2,1)}), bf16[16,2048]{1,0:T(8,128)(2,1)}) %reduce-scatter.17.cloned.1.call-update) | async-done | bytes 65552 | tf_op jit(solution)/shard_map/reduce_scatter | solution.py:174
  1029.0 156.1 %reduce-scatter.13.cloned.1.call-done = bf16[32,512]{1,0:T(8,128)(2,1)} async-done(((bf16[1024,512]{1,0:T(8,128)(2,1)}), bf16[32,512]{1,0:T(8,128)(2,1)}) %reduce-scatter.13.cloned.1.call-update) | async-done | bytes 32784 | tf_op jit(solution)/shard_map/reduce_scatter | solution.py:168
  1186.5 158.7 %reduce-scatter.15.cloned.1.call-done = bf16[32,512]{1,0:T(8,128)(2,1)} async-done(((bf16[1024,512]{1,0:T(8,128)(2,1)}), bf16[32,512]{1,0:T(8,128)(2,1)}) %reduce-scatter.15.cloned.1.call-update) | async-done | bytes 32784 | tf_op jit(solution)/shard_map/reduce_scatter | solution.py:171
  (162 shorter events, 97.9 us)
Async XLA Ops:
  7.2 266.7 %copy-start = (bf16[1,512,2048]{2,1,0:T(8,128)(2,1)S(1)}, bf16[1,512,2048]{2,1,0:T(8,128)(2,1)}, u32[]{:S(2)}) copy-start(bf16[1,512,2048]{2,1,0:T(8,128)(2,1)} %param.17) | copy-start | bytes 6291460
  7.2 3.7 copy-start.2
  7.2 216.8 %all-gather.2.cloned.1.call-start = ((), (), s32[]{:S(2)}) async-start(), calls=%async_computation.7 | async-start | bytes 4595712 | tf_op jit(solution)/shard_map/all_gather | solution.py:80
  8.5 7.4 copy-start.9
  12.7 0.8 copy-start.3
  18.7 9.6 copy-start.7
  18.7 75.4 %all-to-all-start = ((bf16[32,136,512]{2,1,0:T(8,128)(2,1)}), bf16[32,136,512]{2,1,0:T(8,128)(2,1)}, u32[]{:S(2)}, u32[]{:S(2)}) async-start(bf16[32,136,512]{2,1,0:T(8,128)(2,1)} %stack.2), calls=%async_computation | async-start | bytes 8912896 | tf_op jit(solution)/shard_map/all_to_all | solution.py:82
  28.2 505.2 %reduce-scatter.19.cloned.1.call-start = ((), (), s32[]{:S(2)}) async-start(), calls=%async_computation.12 | async-start | bytes 4595712
  28.3 4.2 copy-start.24
  31.4 0.8 copy-start.5
  230.4 9.2 copy-start.22
  271.3 0.7 copy-start.20
  272.2 0.7 copy-start.10
  276.4 0.7 copy-start.16
  276.4 0.8 copy-start.18
  363.8 338.4 %reduce-scatter.21.cloned.1.call-start = ((), (), s32[]{:S(2)}) async-start(), calls=%async_computation.13 | async-start | bytes 4595712
  370.3 1.0 copy-start.6
  370.3 1.2 copy-start.13
  370.4 493.5 %reduce-scatter.11.cloned.1.call-start = ((), (), s32[]{:S(2)}) async-start(), calls=%async_computation.8 | async-start | bytes 1081344 | tf_op jit(solution)/shard_map/reduce_scatter | solution.py:165
  371.5 1.9 copy-start.14
  371.5 1.9 copy-start.17
  371.5 1.9 copy-start.19
  373.3 161.1 %copy-start.4 = (f32[136,8,64]{0,2,1:T(8,128)S(1)}, f32[136,8,64]{0,2,1:T(8,128)}, u32[]{:S(2)}) copy-start(f32[136,8,64]{0,2,1:T(8,128)} %copy-done.3) | copy-start | bytes 835588
  373.3 652.5 %reduce-scatter.17.cloned.1.call-start = ((), (), s32[]{:S(2)}) async-start(), calls=%async_computation.11 | async-start | bytes 2162688 | tf_op jit(solution)/shard_map/reduce_scatter | solution.py:174
  375.5 161.5 %copy-start.8 = (bf16[1,1024,512]{2,1,0:T(8,128)(2,1)S(1)}, bf16[1,1024,512]{2,1,0:T(8,128)(2,1)}, u32[]{:S(2)}) copy-start(bf16[1,1024,512]{2,1,0:T(8,128)(2,1)} %param.14) | copy-start | bytes 3145732
  375.5 809.6 %reduce-scatter.13.cloned.1.call-start = ((), (), s32[]{:S(2)}) async-start(), calls=%async_computation.9 | async-start | bytes 1081344 | tf_op jit(solution)/shard_map/reduce_scatter | solution.py:168
  534.7 0.7 copy-start.11
  536.9 0.9 copy-start.12
  536.9 808.3 %reduce-scatter.15.cloned.1.call-start = ((), (), s32[]{:S(2)}) async-start(), calls=%async_computation.10 | async-start | bytes 1081344 | tf_op jit(solution)/shard_map/reduce_scatter | solution.py:171
  537.8 166.2 %copy-start.15 = (bf16[1,136,1024]{2,1,0:T(8,128)(2,1)S(1)}, bf16[1,136,1024]{2,1,0:T(8,128)(2,1)}, u32[]{:S(2)}) copy-start(bf16[1,136,1024]{2,1,0:T(8,128)(2,1)} %param.13) | copy-start | bytes 835588
  702.1 5.7 copy-start.21
  704.0 18.6 %copy-start.23 = (s32[1,136]{1,0:T(1,128)S(1)}, s32[1,136]{1,0:T(1,128)}, u32[]{:S(2)}) copy-start(s32[1,136]{1,0:T(1,128)} %param.19) | copy-start | bytes 1636
  704.3 3.5 collective-permute-start
  707.8 6.7 collective-permute-start.1
  707.8 638.8 %copy-start.1 = (bf16[1,512,2048]{2,1,0:T(8,128)(2,1)S(1)}, bf16[1,512,2048]{2,1,0:T(8,128)(2,1)}, u32[]{:S(2)}) copy-start(bf16[1,512,2048]{2,1,0:T(8,128)(2,1)} %param.17) | copy-start | bytes 6291460
  714.5 8.1 collective-permute-start.2
  722.7 7.0 collective-permute-start.3
  729.6 135.6 %collective-permute-start.4 = (bf16[136,1024]{1,0:T(8,128)(2,1)S(1)}, bf16[136,1024]{1,0:T(8,128)(2,1)S(1)}, u32[]{:S(2)}, u32[]{:S(2)}) collective-permute-start(bf16[136,1024]{1,0:T(8,128)(2,1)S(1)} %collective-permute-done.3), channel_id=1, source_target_pairs={{0,8},{8,0},{1,9},{9,1},{2,10},{10,2},{3,11},{11,3},{4,12},{12,4},... | collective-permute-start | bytes 835592 | tf_op jit(solution)/shard_map/ppermute | solution.py:18
  865.3 162.1 %collective-permute-start.5 = (bf16[136,1024]{1,0:T(8,128)(2,1)S(1)}, bf16[136,1024]{1,0:T(8,128)(2,1)S(1)}, u32[]{:S(2)}, u32[]{:S(2)}) collective-permute-start(bf16[136,1024]{1,0:T(8,128)(2,1)S(1)} %collective-permute-done.4), channel_id=1, source_target_pairs={{0,16},{16,0},{1,17},{17,1},{2,18},{18,2},{3,19},{19,3},{4,20},{20... | collective-permute-start | bytes 835592 | tf_op jit(solution)/shard_map/ppermute | solution.py:18
Sparse Core Ops, SparseCore 0:
  16.1 207.8 all-gather.1
  363.9 169.4 reduce-scatter.18
  535.9 166.1 reduce-scatter.20
  704.3 159.5 reduce-scatter.10
  866.2 159.5 reduce-scatter.16
  1028.1 157.0 reduce-scatter.12
  1187.6 157.5 reduce-scatter.14
